TPU v7x, 32 devices: a whole 2x2x4 slice. The times are simulated.
32 devices in a mesh: fsdp: 8 (over z, y), ctx: 2 (over x), tp: 2 (over core).
Axes of the slice: x: 2, y: 2, z: 4, core: 2. Of those that a mesh axis runs over, the one named last changes fastest.
Arguments:
- tokens: bfloat16 [8, 2, 1280, 768], P('fsdp', 'ctx'), may hold values from -6 to 6
- cotangent: bfloat16 [8, 2, 1280, 768], P('fsdp', 'ctx'), may hold values from -6 to 6
- routes: int32 [8, 2, 1280, 1], P('fsdp', 'ctx', 'tp'), may hold values from 0 to 15; in each aligned block of 640 rows (0 to 639, 640 to 1279, ..., all dimensions but the last counted through in order) at most 80 rows name the same one
- qkv_weight: bfloat16 [3, 768, 768], P(None, 'fsdp', 'tp'), may hold values from -0.3125 to 0.3125
- out_weight: bfloat16 [768, 768], P('tp', 'fsdp'), may hold values from -0.625 to 0.625
- layer_norm_gains: float32 [2, 768], replicated, may hold values from 0.5 to 1.5
- layer_norm_biases: float32 [2, 768], replicated, may hold values from -2 to 2
- up_weight: bfloat16 [16, 768, 3072], P('fsdp', ('ctx', 'tp')), may hold values from -0.21875 to 0.21875
- up_shift: bfloat16 [16, 3072], P('fsdp', ('ctx', 'tp')), may hold values from -2 to 2
- down_weight: bfloat16 [16, 3072, 768], P('fsdp', ('ctx', 'tp')), may hold values from -0.3125 to 0.3125
- down_shift: bfloat16 [16, 768], P('fsdp', ('ctx', 'tp')), may hold values from -2 to 2
- centroids: bfloat16 [16, 768], P('fsdp', ('ctx', 'tp')), may hold values from -0.15625 to 0.15625
Outputs:
- mixed: bfloat16 [8, 2, 1280, 768], P('fsdp', 'ctx')
- tokens_grad: float32 [8, 2, 1280, 768], P('fsdp', 'ctx')
- qkv_grad: float32 [3, 768, 768], P(None, ('fsdp', 'ctx'), 'tp')
- out_grad: float32 [768, 768], P('tp', ('fsdp', 'ctx'))
- gains_grad: float32 [2, 768], P(None, ('fsdp', 'ctx'))
- shifts_grad: float32 [2, 768], P(None, ('fsdp', 'ctx'))
- up_grad: float32 [16, 768, 3072], P('fsdp', ('ctx', 'tp'))
- up_shift_grad: float32 [16, 3072], P('fsdp', ('ctx', 'tp'))
- down_grad: float32 [16, 3072, 768], P('fsdp', ('ctx', 'tp'))
- down_shift_grad: float32 [16, 768], P('fsdp', ('ctx', 'tp'))
- centroids_grad: float32 [16, 768], P('fsdp', ('ctx', 'tp'))
Inputs may be any that keep to these rules, and one draw needn't show every extreme that they name: `routes`: in each aligned block of 640 tokens (the tokens of dimension 2 taken in halves of a block, in order), no expert is named more than 80 times, a bound that some block reaches.
All inputs are finite; a program needn't handle non-finite values.
Results may differ from a plain program's by a relative error of at most 0.024.
Values may be sent and summed in bfloat16 or wider, within the bound.
No kernel may reach another device: no remote copies, remote signals or barrier semaphores. Data moves between devices by JAX's collectives and lax.ppermute only.
A program may use at most 256 MiB of HBM per device.

v0:
```python
from functools import partial
import jax
import jax.numpy as jnp
from jax import lax
from jax.sharding import PartitionSpec as P

HEAD_DIM = 64
PROMPT = 2048
LEN = 256
EPS = 1e-05
NEG = -1e30


def norm_input_rows(values, gain, shift):
    mean = jnp.mean(values, axis=-1, keepdims=True)
    centred = values - mean
    spread = lax.rsqrt(jnp.mean(centred * centred, axis=-1, keepdims=True) + EPS)
    normed = centred * spread
    return (normed * gain + shift, normed, spread)


def norm_back(upstream, normed, spread, gain):
    scaled = upstream * gain
    inner = (
        scaled
        - jnp.mean(scaled, axis=-1, keepdims=True)
        - normed * jnp.mean(scaled * normed, axis=-1, keepdims=True)
    )
    return (spread * inner, jnp.sum(upstream * normed, axis=0), jnp.sum(upstream, axis=0))


def allowed_keys(place, pslice, prompt, length):
    shape = (pslice + length, prompt + length)
    rows = lax.broadcasted_iota(jnp.int32, shape, 0)
    cols = lax.broadcasted_iota(jnp.int32, shape, 1)
    prompt_row = rows < pslice
    prompt_col = cols < prompt
    early = prompt_row & prompt_col & (cols <= place * pslice + rows)
    later = jnp.logical_not(prompt_row) & (prompt_col | (cols - prompt <= rows - pslice))
    return early | later


def dense_weights(qkv_weight, out_weight):
    return (
        lax.all_gather(qkv_weight, "fsdp", axis=1, tiled=True),
        lax.all_gather(out_weight, "fsdp", axis=1, tiled=True),
    )


def expert_weights(up_weight, down_weight, up_shift, down_shift, centroids):
    return (
        lax.all_gather(up_weight, ("ctx", "tp"), axis=1, tiled=True),
        lax.all_gather(down_weight, ("ctx", "tp"), axis=1, tiled=True),
        lax.all_gather(up_shift, ("ctx", "tp"), axis=1, tiled=True),
        lax.all_gather(down_shift, ("ctx", "tp"), axis=1, tiled=True),
        lax.all_gather(centroids, ("ctx", "tp"), axis=1, tiled=True),
    )


def tp_rows(rows):
    return lax.all_gather(rows, "tp", axis=0, tiled=True)


def head_total(terms):
    return lax.psum(terms.astype(jnp.bfloat16), "tp").astype(jnp.float32)


def split_heads(matrix):
    return matrix.reshape(matrix.shape[0], -1, HEAD_DIM).transpose(1, 0, 2)


def join_heads(stacked):
    return stacked.transpose(1, 0, 2).reshape(stacked.shape[1], -1)


def head_forward(allowed, scale, parts):
    query, keys, values = parts
    raw = jnp.einsum("qd,kd->qk", query, keys, preferred_element_type=jnp.float32) * scale
    scores = jnp.where(allowed, raw, NEG)
    top = jnp.max(scores, axis=-1, keepdims=True)
    weights = jnp.exp(scores - top)
    total = jnp.sum(weights, axis=-1, keepdims=True)
    shares = (weights / total).astype(jnp.bfloat16)
    context = jnp.dot(shares, values, preferred_element_type=jnp.float32).astype(jnp.bfloat16)
    return (context, (top + jnp.log(total))[:, 0])


def head_backward(allowed, scale, parts):
    query, keys, values, context_grad, log_total = parts
    raw = jnp.einsum("qd,kd->qk", query, keys, preferred_element_type=jnp.float32) * scale
    scores = jnp.where(allowed, raw, NEG)
    weights = jnp.exp(scores - log_total[:, None])
    values_grad = jnp.einsum(
        "qk,qd->kd", weights.astype(jnp.bfloat16), context_grad, preferred_element_type=jnp.float32
    )
    weight_grad = jnp.einsum("qd,kd->qk", context_grad, values, preferred_element_type=jnp.float32)
    row_dot = jnp.sum(weights * weight_grad, axis=-1, keepdims=True)
    logit_grad = (weights * (weight_grad - row_dot)).astype(jnp.bfloat16)
    query_grad = jnp.dot(logit_grad, keys, preferred_element_type=jnp.float32) * scale
    keys_grad = (
        jnp.einsum("qk,qd->kd", logit_grad, query, preferred_element_type=jnp.float32) * scale
    )
    return (query_grad, keys_grad, values_grad)


def shards(
    tokens,
    cotangent,
    routes,
    qkv_weight,
    out_weight,
    layer_norm_gains,
    layer_norm_biases,
    up_weight,
    up_shift,
    down_weight,
    down_shift,
    centroids,
):
    block = tokens.shape[2]
    width = tokens.shape[3]
    pslice = block - LEN
    half = routes.shape[2]
    place = lax.axis_index("ctx")
    half_start = lax.axis_index("tp") * half
    scale = HEAD_DIM ** (-0.5)
    residual_stream = tokens.reshape(block, width).astype(jnp.float32)
    project_full, output_full = dense_weights(qkv_weight, out_weight)
    first_normed_rows, first_standardized, first_deviation = norm_input_rows(
        residual_stream, layer_norm_gains[0], layer_norm_biases[0]
    )
    first = first_normed_rows.astype(jnp.bfloat16)
    projected = jnp.einsum(
        "rd,jde->jre", first, project_full, preferred_element_type=jnp.float32
    ).astype(jnp.bfloat16)
    queries, keys_own, values_own = (projected[0], projected[1], projected[2])
    prompt_keys, prompt_values = (
        lax.all_gather(keys_own[:pslice], "ctx", axis=0, tiled=True),
        lax.all_gather(values_own[:pslice], "ctx", axis=0, tiled=True),
    )
    keys_all = jnp.concatenate([prompt_keys, keys_own[pslice:]], axis=0)
    values_all = jnp.concatenate([prompt_values, values_own[pslice:]], axis=0)
    allowed = allowed_keys(place, pslice, PROMPT, LEN)
    query_heads = split_heads(queries)
    key_heads = split_heads(keys_all)
    value_heads = split_heads(values_all)
    context_heads, log_total = lax.map(
        partial(head_forward, allowed, scale), (query_heads, key_heads, value_heads)
    )
    context = join_heads(context_heads)
    attended = head_total(jnp.dot(context, output_full, preferred_element_type=jnp.float32))
    residual_rows = residual_stream + attended
    second_normed_rows, second_standardized, second_deviation = norm_input_rows(
        residual_rows, layer_norm_gains[1], layer_norm_biases[1]
    )
    second = second_normed_rows.astype(jnp.bfloat16)
    own_rows = lax.dynamic_slice_in_dim(second, half_start, half, 0)
    route = routes.reshape(half)
    local_experts = up_weight.shape[0]
    owners = lax.axis_size("fsdp")
    total_experts = local_experts * owners
    capacity = 2 * half // total_experts
    slots = total_experts * capacity
    member = (route[:, None] == lax.broadcasted_iota(jnp.int32, (half, total_experts), 1)).astype(
        jnp.int32
    )
    rank = jnp.sum((jnp.cumsum(member, axis=0) - 1) * member, axis=1)
    slot_of = route * capacity + rank
    placing = (lax.broadcasted_iota(jnp.int32, (slots, half), 0) == slot_of[None, :]).astype(
        jnp.bfloat16
    )
    outgoing = (
        jnp.dot(placing, own_rows, preferred_element_type=jnp.float32)
        .astype(jnp.bfloat16)
        .reshape(owners, local_experts, capacity, width)
    )
    up_full, down_full, up_bias, down_bias, centres = expert_weights(
        up_weight, down_weight, up_shift, down_shift, centroids
    )
    arrived = lax.all_to_all(outgoing, "fsdp", split_axis=0, concat_axis=0, tiled=True)
    score = jnp.einsum("sekd,ed->sek", arrived, centres, preferred_element_type=jnp.float32)
    gate = jax.nn.sigmoid(score)
    inner = jnp.einsum(
        "sekd,edf->sekf", arrived, up_full, preferred_element_type=jnp.float32
    ) + up_bias[None, :, None, :].astype(jnp.float32)
    hidden = jax.nn.gelu(inner, approximate=False).astype(jnp.bfloat16)
    result = jnp.einsum(
        "sekf,efd->sekd", hidden, down_full, preferred_element_type=jnp.float32
    ) + down_bias[None, :, None, :].astype(jnp.float32)
    sent = (gate[..., None] * result).astype(jnp.bfloat16)
    returned = lax.all_to_all(sent, "fsdp", split_axis=0, concat_axis=0, tiled=True)
    returned, arrived, inner, hidden, gate, result = (
        returned,
        arrived,
        inner,
        hidden,
        gate,
        result,
    )
    back_rows = jnp.einsum(
        "sr,sd->rd", placing, returned.reshape(slots, width), preferred_element_type=jnp.float32
    ).astype(jnp.bfloat16)
    expert_out = tp_rows(back_rows)
    mixed = (residual_rows + expert_out.astype(jnp.float32)).astype(jnp.bfloat16)
    project_back, output_back = dense_weights(qkv_weight, out_weight)
    up_back, down_back, unused_up, unused_down, centre_back = expert_weights(
        up_weight, down_weight, up_shift, down_shift, centroids
    )
    upstream_rows = cotangent.reshape(block, width)
    upstream = upstream_rows.astype(jnp.float32)
    upstream_half = lax.dynamic_slice_in_dim(upstream_rows, half_start, half, 0)
    grad_out = (
        jnp.dot(placing, upstream_half, preferred_element_type=jnp.float32)
        .astype(jnp.bfloat16)
        .reshape(owners, local_experts, capacity, width)
    )
    arrived_grad = lax.all_to_all(grad_out, "fsdp", split_axis=0, concat_axis=0, tiled=True).astype(
        jnp.float32
    )
    result_grad = (gate[..., None] * arrived_grad).astype(jnp.bfloat16)
    gate_grad = jnp.sum(arrived_grad * result, axis=-1)
    score_grad = (gate_grad * gate * (1.0 - gate)).astype(jnp.bfloat16)
    hidden_grad = jnp.einsum(
        "sekd,efd->sekf", result_grad, down_back, preferred_element_type=jnp.float32
    )
    gelu_pull = jax.vjp(partial(jax.nn.gelu, approximate=False), inner)[1]
    inner_grad = gelu_pull(hidden_grad)[0].astype(jnp.bfloat16)
    rows_grad = jnp.einsum(
        "sekf,edf->sekd", inner_grad, up_back, preferred_element_type=jnp.float32
    )
    rows_grad = rows_grad + score_grad.astype(jnp.float32)[..., None] * centre_back[
        None, :, None, :
    ].astype(jnp.float32)
    sent_grad = lax.all_to_all(
        rows_grad.astype(jnp.bfloat16), "fsdp", split_axis=0, concat_axis=0, tiled=True
    )
    up_local = jnp.einsum("sekd,sekf->edf", arrived, inner_grad, preferred_element_type=jnp.float32)
    down_local = jnp.einsum(
        "sekf,sekd->efd", hidden, result_grad, preferred_element_type=jnp.float32
    )
    up_shift_local = jnp.sum(inner_grad.astype(jnp.float32), axis=(0, 2))
    down_shift_local = jnp.sum(result_grad.astype(jnp.float32), axis=(0, 2))
    centre_local = jnp.einsum(
        "sek,sekd->ed", score_grad, arrived, preferred_element_type=jnp.float32
    )
    up_grad, down_grad, up_shift_grad, down_shift_grad, centroids_grad = (
        lax.psum_scatter(
            up_local.astype(jnp.bfloat16), ("ctx", "tp"), scatter_dimension=1, tiled=True
        ).astype(jnp.float32),
        lax.psum_scatter(
            down_local.astype(jnp.bfloat16), ("ctx", "tp"), scatter_dimension=1, tiled=True
        ).astype(jnp.float32),
        lax.psum_scatter(
            up_shift_local.astype(jnp.bfloat16), ("ctx", "tp"), scatter_dimension=1, tiled=True
        ).astype(jnp.float32),
        lax.psum_scatter(
            down_shift_local.astype(jnp.bfloat16), ("ctx", "tp"), scatter_dimension=1, tiled=True
        ).astype(jnp.float32),
        lax.psum_scatter(
            centre_local.astype(jnp.bfloat16), ("ctx", "tp"), scatter_dimension=1, tiled=True
        ).astype(jnp.float32),
    )
    half_grad = jnp.einsum(
        "sr,sd->rd", placing, sent_grad.reshape(slots, width), preferred_element_type=jnp.float32
    ).astype(jnp.bfloat16)
    second_norm_gradient = tp_rows(half_grad).astype(jnp.float32)
    resid_norm_grad, gain_two_grad, shift_two_grad = norm_back(
        second_norm_gradient, second_standardized, second_deviation, layer_norm_gains[1]
    )
    resid_grad = upstream + resid_norm_grad
    attended_grad = resid_grad.astype(jnp.bfloat16)
    output_grad = jnp.einsum(
        "rh,rd->hd", context, attended_grad, preferred_element_type=jnp.float32
    )
    context_grad = jnp.einsum(
        "rd,hd->rh", attended_grad, output_back, preferred_element_type=jnp.float32
    ).astype(jnp.bfloat16)
    query_grad, keys_grad, values_grad = lax.map(
        partial(head_backward, allowed, scale),
        (query_heads, key_heads, value_heads, split_heads(context_grad), log_total),
    )
    keys_flat = join_heads(keys_grad)
    values_flat = join_heads(values_grad)
    prompt_key_grad, prompt_value_grad = (
        lax.psum_scatter(
            keys_flat[:PROMPT].astype(jnp.bfloat16), "ctx", scatter_dimension=0, tiled=True
        ).astype(jnp.float32),
        lax.psum_scatter(
            values_flat[:PROMPT].astype(jnp.bfloat16), "ctx", scatter_dimension=0, tiled=True
        ).astype(jnp.float32),
    )
    keys_total = jnp.concatenate([prompt_key_grad, keys_flat[PROMPT:]], axis=0).astype(jnp.bfloat16)
    values_total = jnp.concatenate([prompt_value_grad, values_flat[PROMPT:]], axis=0).astype(
        jnp.bfloat16
    )
    queries_total = join_heads(query_grad).astype(jnp.bfloat16)
    stacked = jnp.stack([queries_total, keys_total, values_total])
    project_grad = jnp.einsum("rd,jre->jde", first, stacked, preferred_element_type=jnp.float32)
    first_norm_gradient = head_total(
        jnp.einsum("jre,jde->rd", stacked, project_back, preferred_element_type=jnp.float32)
    )
    stream_norm_grad, gain_one_grad, shift_one_grad = norm_back(
        first_norm_gradient, first_standardized, first_deviation, layer_norm_gains[0]
    )
    tokens_grad = resid_grad + stream_norm_grad
    gains_local = jnp.stack([gain_one_grad, gain_two_grad])
    shifts_local = jnp.stack([shift_one_grad, shift_two_grad])
    qkv_grad, out_grad, gains_grad, shifts_grad = (
        lax.psum_scatter(project_grad, ("fsdp", "ctx"), scatter_dimension=1, tiled=True),
        lax.psum_scatter(output_grad, ("fsdp", "ctx"), scatter_dimension=1, tiled=True),
        lax.psum_scatter(gains_local, ("fsdp", "ctx"), scatter_dimension=1, tiled=True),
        lax.psum_scatter(shifts_local, ("fsdp", "ctx"), scatter_dimension=1, tiled=True),
    )
    return (
        mixed.reshape(1, 1, block, width),
        tokens_grad.reshape(1, 1, block, width),
        qkv_grad,
        out_grad,
        gains_grad,
        shifts_grad,
        up_grad,
        up_shift_grad,
        down_grad,
        down_shift_grad,
        centroids_grad,
    )


def solution(mesh):
    in_specs = (
        P("fsdp", "ctx", None, None),
        P("fsdp", "ctx", None, None),
        P("fsdp", "ctx", "tp", None),
        P(None, "fsdp", "tp"),
        P("tp", "fsdp"),
        P(),
        P(),
        P("fsdp", ("ctx", "tp"), None),
        P("fsdp", ("ctx", "tp")),
        P("fsdp", ("ctx", "tp"), None),
        P("fsdp", ("ctx", "tp")),
        P("fsdp", ("ctx", "tp")),
    )
    out_specs = (
        P("fsdp", "ctx", None, None),
        P("fsdp", "ctx", None, None),
        P(None, ("fsdp", "ctx"), "tp"),
        P("tp", ("fsdp", "ctx")),
        P(None, ("fsdp", "ctx")),
        P(None, ("fsdp", "ctx")),
        P("fsdp", ("ctx", "tp"), None),
        P("fsdp", ("ctx", "tp")),
        P("fsdp", ("ctx", "tp"), None),
        P("fsdp", ("ctx", "tp")),
        P("fsdp", ("ctx", "tp")),
    )
    return jax.shard_map(shards, mesh=mesh, in_specs=in_specs, out_specs=out_specs, check_vma=False)
```

profile of v0, /device:TPU:0, one launch (start us, length us, event | category | flops | bytes accessed | tf_op | source)
XLA Modules:
  0.0 1489.0 jit_solution(16068740951477841922)
XLA Ops:
  14.4 45.3 %all-gather.12.cloned.1.call-done = bf16[3,768,384]{2,1,0:T(8,128)(2,1)} async-done(((bf16[3,96,384]{2,1,0:T(8,128)(2,1)}), bf16[3,768,384]{2,1,0:T(8,128)(2,1)}) %all-gather.12.cloned.1.call-update) | async-done | bytes 1769488 | tf_op jit(solution)/shard_map/all_gather | solution.py:45
  70.2 34.0 %all_gather.41 = bf16[384,768]{0,1:T(8,128)(2,1)} all-gather(bf16[384,96]{0,1:T(8,128)(2,1)S(1)} %copy-done.25), channel_id=1, replica_groups=mesh['fsdp'=8,'ctx'=2,'tp'=2] {'fsdp'}, dimensions={1}, use_global_device_ids=true | all-gather | bytes 663552 | tf_op jit(solution)/shard_map/all_gather | solution.py:46
  111.3 11.0 all-gather.24.cloned.1.call-done
  130.0 82.3 %while.28 = (s32[]{:T(128)}, bf16[6,1280,64]{1,2,0:T(8,128)(2,1)}, f32[6,1280]{1,0:T(8,128)}, bf16[6,1280,64]{2,1,0:T(8,128)(2,1)}, bf16[6,2304,64]{2,1,0:T(8,12...) while((s32[]{:T(128)}, bf16[6,1280,64]{1,2,0:T(8,128)(2,1)}, ...), condition=%wide.region_5.6_spmd.clone, body=%wide.region_2.5_spmd.clone.sunk | while | flops 799292160 | bytes 37163152 | solution.py:147
  130.0 6.9 fusion.199
  143.7 6.9 fusion.199
  157.4 6.9 fusion.199
  171.1 6.9 fusion.199
  184.8 6.9 fusion.199
  198.5 6.9 fusion.199
  221.1 18.6 %all-reduce.5.cloned.1.call-done = bf16[1280,768]{1,0:T(8,128)(2,1)} async-done(((bf16[1280,768]{1,0:T(8,128)(2,1)}), bf16[1280,768]{1,0:T(8,128)(2,1)}) %all-reduce.5.cloned.1.call-update) | async-done | bytes 1966096 | tf_op jit(solution)/shard_map/psum | solution.py:65
  248.6 5.7 all-to-all-start
  254.3 5.4 all_gather.44
  259.7 5.2 all-gather.2
  265.0 5.2 all-gather.3
  273.9 26.3 %all-to-all-done = bf16[8,2,80,768]{3,2,1,0:T(8,128)(2,1)} async-done(((bf16[8,2,80,768]{3,2,1,0:T(8,128)(2,1)}), bf16[8,2,80,768]{3,2,1,0:T(8,128)(2,1)}, u32[]{:S(2)}, u32[]{:S(2)}) %all-to-all-start) | async-done | bytes 1966112 | tf_op jit(solution)/shard_map/all_to_all | solution.py:180
  306.3 43.6 %fusion.66 = (bf16[8,2,80,3072]{3,2,0,1:T(8,128)(2,1)}, f32[8,2,80,3072]{3,2,0,1:T(8,128)}, f32[2,8,80,3072]{3,2,1,0:T(8,128)}) fusion(f32[2,3072]{1,0:T(2,128)S(1)} %convert_element_type.197, bf16[2,768,3072]{2,1,0:T(8,128)(2,1)} %all-gather.14.cloned.1.call-done, bf16[8,2,80,768]{3,2,1,0:T(8,128)(2,1)} %all-to-all-done), kind=kOutput, calls=%fused_computation.82 | convolution fusion | flops 6299320320 | bytes 50749440 | tf_op jit(solution)/shard_map/sekd,edf->sekf/dot_general | solution.py:183
  349.9 13.3 fusion.110
  363.8 23.0 %fusion.167 = (bf16[2,3072]{1,0:T(2,128)(2,1)}, bf16[8,2,80,3072]{3,2,0,1:T(8,128)(2,1)}) fusion(f32[8,2,80,3072]{3,2,0,1:T(8,128)} %get-tuple-element.291, bf16[2,3072,768]{2,1,0:T(8,128)(2,1)} %all-gather.16.cloned.1.call-done, f32[8,2,80]{2,0,1:T(8,128)S(1)} %divide_bitcast_fusion, bf16[8,2,80,768]{3,2,1,0:T(8,128)(2,1)S(1)} %all-to-all-done.2, ...), kind=kOutput, calls=%fused_computation.234 | convolution fusion | flops 6105655296 | bytes 50766848 | tf_op jit(solution)/shard_map/sekd,efd->sekf/dot_general | solution.py:223
  386.8 11.4 fusion.118
  398.4 51.3 %all_to_all.20 = bf16[8,2,80,768]{3,2,1,0:T(8,128)(2,1)S(1)} all-to-all(bf16[8,2,80,768]{3,2,1,0:T(8,128)(2,1)S(1)} %copy.90), channel_id=1, replica_groups=mesh['fsdp'=8,'ctx'=2,'tp'=2] {'fsdp'}, dimensions={0} | all-to-all | bytes 3932160 | tf_op jit(solution)/shard_map/all_to_all | solution.py:234
  452.4 9.1 all-gather.20.cloned.1.call-done
  461.6 4.8 fusion.116
  475.3 139.5 %while.29 = (s32[]{:T(128)}, bf16[6,1280,64]{1,2,0:T(8,128)(2,1)}, bf16[6,2304,64]{1,2,0:T(8,128)(2,1)}, bf16[6,2304,64]{1,2,0:T(8,128)(2,1)}, bf16[6,1280,64]{2...) while((s32[]{:T(128)}, bf16[6,1280,64]{1,2,0:T(8,128)(2,1)}, ...), condition=%wide.region_17.18_spmd.clone, body=%wide.region_15.17_spmd.clone.sunk | while | flops 1934850816 | bytes 107280608 | solution.py:278
  479.0 8.8 multiply_reduce_fusion.3
  502.2 8.8 multiply_reduce_fusion.3
  525.4 8.8 multiply_reduce_fusion.3
  548.6 8.8 multiply_reduce_fusion.3
  571.8 8.8 multiply_reduce_fusion.3
  594.9 8.8 multiply_reduce_fusion.3
  622.6 5.8 all-to-all-start.1
  631.3 14.0 reduce-scatter.23.cloned.1.call-done
  645.3 29.0 %reduce-scatter.21.cloned.1.call-done = bf16[1024,384]{1,0:T(8,128)(2,1)} async-done(((bf16[2048,384]{1,0:T(8,128)(2,1)}), bf16[1024,384]{1,0:T(8,128)(2,1)}) %reduce-scatter.21.cloned.1.call-update) | async-done | bytes 786448 | tf_op jit(solution)/shard_map/reduce_scatter | solution.py:285
  674.3 6.1 bitcast_convert_fusion.2
  690.8 10.9 all-reduce.7.cloned.1.call-done
  707.2 5.9 convolution_bitcast_fusion
  713.1 6.2 copy.98
  719.4 13.2 bitcast_convert_fusion.1
  732.6 13.2 bitcast_convert_fusion
  747.0 4.4 fusion.148
  757.3 6.4 fusion.107
  763.7 117.0 %reduce-scatter.31.cloned.1.call-done = f32[48,2]{1,0:T(8,128)} async-done(((f32[768,2]{1,0:T(8,128)}), f32[48,2]{1,0:T(8,128)}) %reduce-scatter.31.cloned.1.call-update) | async-done | bytes 400
  882.0 125.4 %reduce-scatter.33.cloned.1.call-done = f32[48,2]{1,0:T(8,128)} async-done(((f32[768,2]{1,0:T(8,128)}), f32[48,2]{1,0:T(8,128)}) %reduce-scatter.33.cloned.1.call-update) | async-done | bytes 400
  1008.8 182.4 %all-reduce.9.cloned.1.call-done = f32[3,768,384]{2,0,1:T(4,128)} async-done(((f32[3,768,384]{2,0,1:T(4,128)}), f32[3,768,384]{2,0,1:T(4,128)}) %all-reduce.9.cloned.1.call-update) | async-done | bytes 3538960
  1192.9 77.6 %reduce-scatter.27.cloned.1.call-done = bf16[2,192,3072]{2,1,0:T(8,128)(2,1)} async-done(((bf16[2,768,3072]{2,1,0:T(8,128)(2,1)}), bf16[2,192,3072]{2,1,0:T(8,128)(2,1)}) %reduce-scatter.27.cloned.1.call-update) | async-done | bytes 2359312 | tf_op jit(solution)/shard_map/reduce_scatter | solution.py:247
  1270.6 4.4 convert_element_type.226
  1275.0 76.0 %reduce-scatter.29.cloned.1.call-done = bf16[2,768,768]{2,1,0:T(8,128)(2,1)} async-done(((bf16[2,3072,768]{2,1,0:T(8,128)(2,1)}), bf16[2,768,768]{2,1,0:T(8,128)(2,1)}) %reduce-scatter.29.cloned.1.call-update) | async-done | bytes 2359312 | tf_op jit(solution)/shard_map/reduce_scatter | solution.py:250
  1355.2 126.0 %reduce-scatter.25.cloned.1.call-done = f32[384,48]{0,1:T(8,128)} async-done(((f32[384,768]{0,1:T(8,128)}), f32[384,48]{0,1:T(8,128)}) %reduce-scatter.25.cloned.1.call-update) | async-done | bytes 73744 | tf_op jit(solution)/shard_map/reduce_scatter | solution.py:310
  (337 shorter events, 239.3 us)
Async XLA Ops:
  8.0 51.7 %copy-start = (bf16[1,1,1280,768]{3,2,1,0:T(8,128)(2,1)S(1)}, bf16[1,1,1280,768]{3,2,1,0:T(8,128)(2,1)}, u32[]{:S(2)}) copy-start(bf16[1,1,1280,768]{3,2,1,0:T(8,128)(2,1)} %param.16) | copy-start | bytes 5898244
  8.0 51.7 %all-gather.12.cloned.1.call-start = ((), (), s32[]{:S(2)}) async-start(), calls=%async_computation.14 | async-start | bytes 1990656 | tf_op jit(solution)/shard_map/all_gather | solution.py:45
  8.8 99.5 %all-gather.22.cloned.1.call-start = ((), (), s32[]{:S(2)}) async-start(), calls=%async_computation.26 | async-start | bytes 2359296 | tf_op jit(solution)/shard_map/all_gather | solution.py:138
  10.2 53.8 %copy-start.28 = (f32[768]{0:T(1024)}, f32[768]{0:T(1024)S(1)}, u32[]{:S(2)}) copy-start(f32[768]{0:T(1024)S(1)} %get-tuple-element.307) | copy-start | bytes 9220
  10.2 53.8 %copy-start.40 = (f32[768]{0:T(1024)}, f32[768]{0:T(1024)S(1)}, u32[]{:S(2)}) copy-start(f32[768]{0:T(1024)S(1)} %get-tuple-element.233) | copy-start | bytes 9220
  12.1 52.0 %copy-start.21 = (f32[1280]{0:T(1024)}, f32[1280]{0:T(1024)S(1)}, u32[]{:S(2)}) copy-start(f32[1280]{0:T(1024)S(1)} %broadcast_multiply_fusion.5) | copy-start | bytes 15364
  14.4 49.7 %copy-start.23 = (f32[1280]{0:T(1024)}, f32[1280]{0:T(1024)S(1)}, u32[]{:S(2)}) copy-start(f32[1280]{0:T(1024)S(1)} %add_rsqrt_fusion.1) | copy-start | bytes 15364
  67.0 37.2 %slice-start = ((bf16[3,1280,384]{1,2,0:T(8,128)(2,1)}), bf16[1,1280,384]{1,2,0:T(8,128)(2,1)S(1)}, s32[]{:S(2)}) async-start(bf16[3,1280,384]{1,2,0:T(8,128)(2,1)} %copy-done.11), calls=%async_computation.34 | async-start | bytes 1966080 | tf_op jit(solution)/shard_map/slice | solution.py:136
  67.1 55.3 %all-gather.24.cloned.1.call-start = ((), (), s32[]{:S(2)}) async-start(), calls=%async_computation.27 | async-start | bytes 2359296 | tf_op jit(solution)/shard_map/all_gather | solution.py:139
  67.8 171.8 %all-reduce.5.cloned.1.call-start = ((), (), s32[]{:S(2)}) async-start(), calls=%async_computation.15 | async-start | bytes 3932160 | tf_op jit(solution)/shard_map/psum | solution.py:65
  212.3 6.3 copy-start.37
  218.0 21.7 %copy-start.1 = (bf16[1,1,1280,768]{3,2,1,0:T(8,128)(2,1)S(1)}, bf16[1,1,1280,768]{3,2,1,0:T(8,128)(2,1)}, u32[]{:S(2)}) copy-start(bf16[1,1,1280,768]{3,2,1,0:T(8,128)(2,1)} %param.16) | copy-start | bytes 5898244
  218.0 88.3 %all-gather.14.cloned.1.call-start = ((), (), s32[]{:S(2)}) async-start(), calls=%async_computation.16 | async-start | bytes 11796480 | tf_op jit(solution)/shard_map/all_gather | solution.py:52
  218.6 131.3 %all-gather.16.cloned.1.call-start = ((), (), s32[]{:S(2)}) async-start(), calls=%async_computation.17 | async-start | bytes 11796480 | tf_op jit(solution)/shard_map/all_gather | solution.py:53
  221.1 49.8 %copy-start.42 = (s32[640]{0:T(1024)}, s32[640]{0:T(1024)S(1)}, u32[]{:S(2)}) copy-start(s32[640]{0:T(1024)S(1)} %multiply_add_fusion) | copy-start | bytes 7684
  248.6 11.1 copy-start.49
  248.6 16.4 %copy-start.50 = (bf16[2,192]{1,0:T(2,128)(2,1)S(1)}, bf16[2,192]{1,0:T(2,128)(2,1)}, u32[]{:S(2)}) copy-start(bf16[2,192]{1,0:T(2,128)(2,1)} %param.26) | copy-start | bytes 2308
  248.6 22.3 %copy-start.13 = (bf16[1,1,1280,768]{3,2,1,0:T(8,128)(2,1)S(1)}, bf16[1,1,1280,768]{3,2,1,0:T(8,128)(2,1)}, u32[]{:S(2)}) copy-start(bf16[1,1,1280,768]{3,2,1,0:T(8,128)(2,1)} %param.17) | copy-start | bytes 5898244
  248.6 51.6 %all-to-all-start = ((bf16[8,2,80,768]{3,2,1,0:T(8,128)(2,1)}), bf16[8,2,80,768]{3,2,1,0:T(8,128)(2,1)}, u32[]{:S(2)}, u32[]{:S(2)}) async-start(bf16[8,2,80,768]{3,2,1,0:T(8,128)(2,1)} %bitcast.381), calls=%async_computation | async-start | bytes 3932160 | tf_op jit(solution)/shard_map/all_to_all | solution.py:180
  300.2 49.7 %all-to-all-start.2 = ((bf16[8,2,80,768]{3,2,1,0:T(8,128)(2,1)}), bf16[8,2,80,768]{3,2,1,0:T(8,128)(2,1)S(1)}, u32[]{:S(2)}, u32[]{:S(2)}) async-start(bf16[8,2,80,768]{3,2,1,0:T(8,128)(2,1)} %bitcast.380), calls=%async_computation.2 | async-start | bytes 3932160 | tf_op jit(solution)/shard_map/all_to_all | solution.py:217
  303.9 157.7 %all-gather.20.cloned.1.call-start = ((), (), s32[]{:S(2)}) async-start(), calls=%async_computation.19 | async-start | bytes 2949120 | tf_op jit(solution)/shard_map/all_gather | solution.py:61
  306.2 57.6 %copy-start.32 = (f32[8,2,80]{2,0,1:T(8,128)}, f32[8,2,80]{2,0,1:T(8,128)S(1)}, u32[]{:S(2)}) copy-start(f32[8,2,80]{2,0,1:T(8,128)S(1)} %divide_bitcast_fusion) | copy-start | bytes 15364
  349.9 13.9 copy-start.9
  363.8 23.0 %copy-start.39 = (f32[2,768]{1,0:T(2,128)S(1)}, f32[2,768]{1,0:T(2,128)}, u32[]{:S(2)}) copy-start(f32[2,768]{1,0:T(2,128)} %bitcast_convert_fusion.4) | copy-start | bytes 18436
  398.2 51.4 %copy-start.43 = (s32[640]{0:T(1024)S(1)}, s32[640]{0:T(1024)}, u32[]{:S(2)}) copy-start(s32[640]{0:T(1024)} %copy-done.42) | copy-start | bytes 7684
  449.7 11.9 copy-start.31
  449.7 16.7 %copy-start.14 = (bf16[1,1,1280,768]{3,2,1,0:T(8,128)(2,1)S(1)}, bf16[1,1,1280,768]{3,2,1,0:T(8,128)(2,1)}, u32[]{:S(2)}) copy-start(bf16[1,1,1280,768]{3,2,1,0:T(8,128)(2,1)} %param.17) | copy-start | bytes 5898244
  452.3 14.0 copy-start.27
  452.4 192.9 %reduce-scatter.23.cloned.1.call-start = ((), (), s32[]{:S(2)}) async-start(), calls=%async_computation.21 | async-start | bytes 2359296 | tf_op jit(solution)/shard_map/reduce_scatter | solution.py:288
  617.8 56.5 %reduce-scatter.21.cloned.1.call-start = ((), (), s32[]{:S(2)}) async-start(), calls=%async_computation.20 | async-start | bytes 2359296 | tf_op jit(solution)/shard_map/reduce_scatter | solution.py:285
  621.2 9.5 copy-start.20
  622.6 63.6 %all-to-all-start.1 = ((bf16[8,2,80,768]{3,2,1,0:T(8,128)(2,1)}), bf16[8,2,80,768]{3,2,1,0:T(8,128)(2,1)}, u32[]{:S(2)}, u32[]{:S(2)}) async-start(bf16[8,2,80,768]{3,2,1,0:T(8,128)(2,1)} %copy.88), calls=%async_computation.1 | async-start | bytes 3932160 | tf_op jit(solution)/shard_map/all_to_all | solution.py:191
  628.4 73.3 %all-reduce.7.cloned.1.call-start = ((), (), s32[]{:S(2)}) async-start(), calls=%async_computation.22 | async-start | bytes 3932160 | tf_op jit(solution)/shard_map/psum | solution.py:65
  680.5 72.2 %reduce-scatter.37.cloned.1.call-start = ((), (), s32[]{:S(2)}) async-start(), calls=%async_computation.31 | async-start | bytes 245760
  681.9 72.3 %reduce-scatter.39.cloned.1.call-start = ((), (), s32[]{:S(2)}) async-start(), calls=%async_computation.32 | async-start | bytes 245760
  684.8 70.8 %reduce-scatter.35.cloned.1.call-start = ((), (), s32[]{:S(2)}) async-start(), calls=%async_computation.30 | async-start | bytes 983040
  686.2 71.2 %all-gather.18.cloned.1.call-start = ((), (), s32[]{:S(2)}) async-start(), calls=%async_computation.18 | async-start | bytes 2949120 | tf_op jit(solution)/shard_map/all_gather | solution.py:61
  686.3 15.4 %copy-start.2 = (bf16[1,1,1280,768]{3,2,1,0:T(8,128)(2,1)S(1)}, bf16[1,1,1280,768]{3,2,1,0:T(8,128)(2,1)}, u32[]{:S(2)}) copy-start(bf16[1,1,1280,768]{3,2,1,0:T(8,128)(2,1)} %param.16) | copy-start | bytes 5898244
  686.3 15.4 %copy-start.22 = (f32[1280]{0:T(1024)S(1)}, f32[1280]{0:T(1024)}, u32[]{:S(2)}) copy-start(f32[1280]{0:T(1024)} %copy-done.21) | copy-start | bytes 15364
  686.3 15.4 %copy-start.24 = (f32[1280]{0:T(1024)S(1)}, f32[1280]{0:T(1024)}, u32[]{:S(2)}) copy-start(f32[1280]{0:T(1024)} %copy-done.23) | copy-start | bytes 15364
  686.3 15.4 %copy-start.29 = (f32[768]{0:T(1024)S(1)}, f32[768]{0:T(1024)}, u32[]{:S(2)}) copy-start(f32[768]{0:T(1024)} %copy-done.28) | copy-start | bytes 9220
  690.6 16.5 %copy-start.41 = (f32[768]{0:T(1024)S(1)}, f32[768]{0:T(1024)}, u32[]{:S(2)}) copy-start(f32[768]{0:T(1024)} %copy-done.40) | copy-start | bytes 9220
  690.7 190.0 %reduce-scatter.31.cloned.1.call-start = ((), (), s32[]{:S(2)}) async-start(), calls=%async_computation.28 | async-start | bytes 417792
  706.1 301.4 %reduce-scatter.33.cloned.1.call-start = ((), (), s32[]{:S(2)}) async-start(), calls=%async_computation.29 | async-start | bytes 417792
  707.1 484.1 %all-reduce.9.cloned.1.call-start = ((), (), s32[]{:S(2)}) async-start(), calls=%async_computation.33 | async-start | bytes 9437184
  719.3 551.2 %reduce-scatter.27.cloned.1.call-start = ((), (), s32[]{:S(2)}) async-start(), calls=%async_computation.24 | async-start | bytes 11796480 | tf_op jit(solution)/shard_map/reduce_scatter | solution.py:247
  732.6 618.4 %reduce-scatter.29.cloned.1.call-start = ((), (), s32[]{:S(2)}) async-start(), calls=%async_computation.25 | async-start | bytes 11796480 | tf_op jit(solution)/shard_map/reduce_scatter | solution.py:250
  745.9 735.3 %reduce-scatter.25.cloned.1.call-start = ((), (), s32[]{:S(2)}) async-start(), calls=%async_computation.23 | async-start | bytes 1253376 | tf_op jit(solution)/shard_map/reduce_scatter | solution.py:310
  (38 other events, 117.4 us)
Sparse Core Ops, SparseCore 0:
  11.0 48.6 all-gather.11
  67.2 25.7 all-gather.21
  95.1 27.1 all-gather.23
  218.1 21.4 all-reduce.4
  452.5 9.0 all-gather.19
  618.0 27.3 reduce-scatter.22
  648.1 26.1 reduce-scatter.20
  680.6 21.0 all-reduce.6
  703.2 11.5 all-gather.17
Sparse Core Ops, SparseCore 1:
  220.0 64.2 all-gather.13
  285.7 64.1 all-gather.15
  684.0 19.8 reduce-scatter.36
  706.3 20.7 reduce-scatter.38
  729.6 23.1 reduce-scatter.34
  757.4 123.2 reduce-scatter.30
  885.2 122.2 reduce-scatter.32
  1013.6 177.5 all-reduce.8
  1193.7 76.8 reduce-scatter.26
  1273.2 77.8 reduce-scatter.28
  1356.2 124.9 reduce-scatter.24
where the time goes:
time: 1500 us; the launch traced here: 1490 us
  waiting for transfers between devices  871 us (58%)
  matrix products  344 us (23%)
  blocking collectives  101 us (7%)
  local copies, waits for them, and re-layouts  73.5 us (5%)
  other arithmetic  64.7 us (4%)
  between operations  17.5 us (1%)
  starting transfers between devices  16 us (1%)
    unnamed x26, waiting for transfers between devices  427 us
    reduce_scatter x1, waiting for transfers between devices, shards(): lax.psum_scatter(output_grad, ('fsdp', 'ctx'), scatter_dimension=1, tiled...  126 us
    reduce_scatter x1, waiting for transfers between devices, shards(): lax.psum_scatter(up_local.astype(jnp.bfloat16), ('ctx', 'tp'), scatter_di...  77.6 us
    reduce_scatter x1, waiting for transfers between devices, shards(): lax.psum_scatter(down_local.astype(jnp.bfloat16), ('ctx', 'tp'), scatter_...  76 us
    dot_general x6, matrix products, head_backward(): jnp.einsum('qd,kd->qk', query, keys, preferred_element_type=jnp.float32)  53 us
    all_to_all x1, blocking collectives, shards(): lax.all_to_all(rows_grad.astype(jnp.bfloat16), 'fsdp', split_axis=0, conc...  51.3 us
    all_gather x1, waiting for transfers between devices, dense_weights(): lax.all_gather(qkv_weight, 'fsdp', axis=1, tiled=True)  45.3 us
    dot_general x1, matrix products, shards(): jnp.einsum('sekd,edf->sekf', arrived, up_full, preferred_element_type=jnp...  43.6 us
  transfers between devices with their start and end apart: 23, of which 14 were waited for; matrix products, arithmetic and copies ran while one was open for 11% of the time, Pallas kernels for 0%

commit v1 on v0

--- a/solution.py
+++ b/solution.py
@@ -43,7 +43,9 @@
 def dense_weights(qkv_weight, out_weight):
     return (
         lax.all_gather(qkv_weight, "fsdp", axis=1, tiled=True),
-        lax.all_gather(out_weight, "fsdp", axis=1, tiled=True),
+        jnp.concatenate(
+            lax.all_to_all(jnp.stack([out_weight] * lax.axis_size("fsdp")), "fsdp", 0, 0), axis=1
+        ),
     )
 
 

time: 1500 us -> 1500 us (level)
  blocking collectives: 101 us -> 67 us
  waiting for transfers between devices: 871 us -> 900 us
    all_gather x1 -> x0, blocking collectives: 34 us -> none  [dense_weights(): lax.all_gather(out_weight, 'fsdp', axis=1, tiled=True)]
    all_gather x1, waiting for transfers between devices: 11 us -> 26.3 us  [shards(): lax.all_gather(values_own[:pslice], 'ctx', axis=0, tiled=True)]
  transfers between devices with their start and end apart: 23 -> 24, of which waited for: 14 -> 15; matrix products, arithmetic and copies ran while one was open for 11% -> 17% of each run, Pallas kernels for 0% -> 0%
where the time goes in v1:
time: 1500 us; the launch traced here: 1490 us
  waiting for transfers between devices  900 us (60%)
  matrix products  344 us (23%)
  local copies, waits for them, and re-layouts  74.3 us (5%)
  blocking collectives  67 us (4%)
  other arithmetic  64.7 us (4%)
  starting transfers between devices  20.6 us (1%)
  between operations  17.6 us (1%)
    unnamed x26, waiting for transfers between devices  428 us
    reduce_scatter x1, waiting for transfers between devices, shards(): lax.psum_scatter(output_grad, ('fsdp', 'ctx'), scatter_dimension=1, tiled...  126 us
    reduce_scatter x1, waiting for transfers between devices, shards(): lax.psum_scatter(up_local.astype(jnp.bfloat16), ('ctx', 'tp'), scatter_di...  77.6 us
    reduce_scatter x1, waiting for transfers between devices, shards(): lax.psum_scatter(down_local.astype(jnp.bfloat16), ('ctx', 'tp'), scatter_...  76 us
    dot_general x6, matrix products, head_backward(): jnp.einsum('qd,kd->qk', query, keys, preferred_element_type=jnp.float32)  53 us
    all_to_all x1, blocking collectives, shards(): lax.all_to_all(rows_grad.astype(jnp.bfloat16), 'fsdp', split_axis=0, conc...  51.3 us
    all_gather x1, waiting for transfers between devices, dense_weights(): lax.all_gather(qkv_weight, 'fsdp', axis=1, tiled=True)  45.3 us
    dot_general x1, matrix products, shards(): jnp.einsum('sekd,edf->sekf', arrived, up_full, preferred_element_type=jnp...  43.7 us
  transfers between devices with their start and end apart: 24, of which 15 were waited for; matrix products, arithmetic and copies ran while one was open for 17% of the time, Pallas kernels for 0%

profile of v1, /device:TPU:0, one launch (start us, length us, event | category | flops | bytes accessed | tf_op | source)
XLA Modules:
  0.0 1489.1 jit_solution(15589165574793478174)
XLA Ops:
  14.4 45.3 %all-gather.12.cloned.1.call-done = bf16[3,768,384]{2,1,0:T(8,128)(2,1)} async-done(((bf16[3,96,384]{2,1,0:T(8,128)(2,1)}), bf16[3,768,384]{2,1,0:T(8,128)(2,1)}) %all-gather.12.cloned.1.call-update) | async-done | bytes 1769488 | tf_op jit(solution)/shard_map/all_gather | solution.py:45
  79.7 13.3 all-gather.22.cloned.1.call-done
  96.1 26.3 %all-gather.24.cloned.1.call-done = bf16[1,2048,384]{1,2,0:T(8,128)(2,1)} async-done(((bf16[1,1024,384]{1,2,0:T(8,128)(2,1)}), bf16[1,2048,384]{1,2,0:T(8,128)(2,1)}) %all-gather.24.cloned.1.call-update) | async-done | bytes 1572880 | tf_op jit(solution)/shard_map/all_gather | solution.py:141
  130.0 82.4 %while.28 = (s32[]{:T(128)}, bf16[6,1280,64]{1,2,0:T(8,128)(2,1)}, f32[6,1280]{1,0:T(8,128)}, bf16[6,1280,64]{2,1,0:T(8,128)(2,1)}, bf16[6,2304,64]{2,1,0:T(8,12...) while((s32[]{:T(128)}, bf16[6,1280,64]{1,2,0:T(8,128)(2,1)}, ...), condition=%wide.region_5.6_spmd.clone, body=%wide.region_2.5_spmd.clone.sunk | while | flops 799292160 | bytes 37163152 | solution.py:149
  130.0 6.9 fusion.199
  143.7 6.9 fusion.199
  157.4 6.9 fusion.199
  171.1 6.9 fusion.199
  184.8 6.9 fusion.199
  198.5 6.9 fusion.199
  221.1 18.6 %all-reduce.5.cloned.1.call-done = bf16[1280,768]{1,0:T(8,128)(2,1)} async-done(((bf16[1280,768]{1,0:T(8,128)(2,1)}), bf16[1280,768]{1,0:T(8,128)(2,1)}) %all-reduce.5.cloned.1.call-update) | async-done | bytes 1966096 | tf_op jit(solution)/shard_map/psum | solution.py:67
  248.6 5.7 all-to-all-start.1
  254.3 5.4 all_gather.39
  259.7 5.2 all-gather.2
  265.0 5.2 all-gather.3
  273.9 26.3 %all-to-all-done.1 = bf16[8,2,80,768]{3,2,1,0:T(8,128)(2,1)} async-done(((bf16[8,2,80,768]{3,2,1,0:T(8,128)(2,1)}), bf16[8,2,80,768]{3,2,1,0:T(8,128)(2,1)}, u32[]{:S(2)}, u32[]{:S(2)}) %all-to-all-start.1) | async-done | bytes 1966112 | tf_op jit(solution)/shard_map/all_to_all | solution.py:182
  306.3 43.7 %fusion.66 = (bf16[8,2,80,3072]{3,2,0,1:T(8,128)(2,1)}, f32[8,2,80,3072]{3,2,0,1:T(8,128)}, f32[2,8,80,3072]{3,2,1,0:T(8,128)}) fusion(f32[2,3072]{1,0:T(2,128)S(1)} %convert_element_type.197, bf16[2,768,3072]{2,1,0:T(8,128)(2,1)} %all-gather.14.cloned.1.call-done, bf16[8,2,80,768]{3,2,1,0:T(8,128)(2,1)} %all-to-all-done.1), kind=kOutput, calls=%fused_computation.82 | convolution fusion | flops 6299320320 | bytes 50749440 | tf_op jit(solution)/shard_map/sekd,edf->sekf/dot_general | solution.py:185
  350.0 13.3 fusion.110
  363.9 23.0 %fusion.167 = (bf16[2,3072]{1,0:T(2,128)(2,1)}, bf16[8,2,80,3072]{3,2,0,1:T(8,128)(2,1)}) fusion(f32[8,2,80,3072]{3,2,0,1:T(8,128)} %get-tuple-element.291, bf16[2,3072,768]{2,1,0:T(8,128)(2,1)} %all-gather.16.cloned.1.call-done, f32[8,2,80]{2,0,1:T(8,128)S(1)} %divide_bitcast_fusion, bf16[8,2,80,768]{3,2,1,0:T(8,128)(2,1)S(1)} %all-to-all-done.3, ...), kind=kOutput, calls=%fused_computation.234 | convolution fusion | flops 6105655296 | bytes 50766848 | tf_op jit(solution)/shard_map/sekd,efd->sekf/dot_general | solution.py:225
  386.9 11.4 fusion.118
  398.4 51.3 %all_to_all.26 = bf16[8,2,80,768]{3,2,1,0:T(8,128)(2,1)S(1)} all-to-all(bf16[8,2,80,768]{3,2,1,0:T(8,128)(2,1)S(1)} %copy.91), channel_id=1, replica_groups=mesh['fsdp'=8,'ctx'=2,'tp'=2] {'fsdp'}, dimensions={0} | all-to-all | bytes 3932160 | tf_op jit(solution)/shard_map/all_to_all | solution.py:236
  452.5 9.1 all-gather.20.cloned.1.call-done
  461.6 4.7 fusion.116
  475.4 139.5 %while.29 = (s32[]{:T(128)}, bf16[6,1280,64]{1,2,0:T(8,128)(2,1)}, bf16[6,2304,64]{1,2,0:T(8,128)(2,1)}, bf16[6,2304,64]{1,2,0:T(8,128)(2,1)}, bf16[6,1280,64]{2...) while((s32[]{:T(128)}, bf16[6,1280,64]{1,2,0:T(8,128)(2,1)}, ...), condition=%wide.region_17.18_spmd.clone, body=%wide.region_15.17_spmd.clone.sunk | while | flops 1934850816 | bytes 107280608 | solution.py:280
  479.1 8.8 multiply_reduce_fusion.3
  502.3 8.8 multiply_reduce_fusion.3
  525.5 8.8 multiply_reduce_fusion.3
  548.7 8.8 multiply_reduce_fusion.3
  571.9 8.8 multiply_reduce_fusion.3
  595.0 8.8 multiply_reduce_fusion.3
  622.7 5.8 all-to-all-start.2
  631.4 14.0 reduce-scatter.23.cloned.1.call-done
  645.4 29.0 %reduce-scatter.21.cloned.1.call-done = bf16[1024,384]{1,0:T(8,128)(2,1)} async-done(((bf16[2048,384]{1,0:T(8,128)(2,1)}), bf16[1024,384]{1,0:T(8,128)(2,1)}) %reduce-scatter.21.cloned.1.call-update) | async-done | bytes 786448 | tf_op jit(solution)/shard_map/reduce_scatter | solution.py:287
  674.5 6.1 bitcast_convert_fusion.2
  690.9 10.9 all-reduce.7.cloned.1.call-done
  707.3 5.9 convolution_bitcast_fusion
  713.2 6.2 copy.99
  719.5 13.0 bitcast_convert_fusion.1
  732.6 13.1 bitcast_convert_fusion
  746.9 4.4 fusion.148
  757.2 6.4 fusion.107
  763.6 117.2 %reduce-scatter.31.cloned.1.call-done = f32[48,2]{1,0:T(8,128)} async-done(((f32[768,2]{1,0:T(8,128)}), f32[48,2]{1,0:T(8,128)}) %reduce-scatter.31.cloned.1.call-update) | async-done | bytes 400
  882.1 125.5 %reduce-scatter.33.cloned.1.call-done = f32[48,2]{1,0:T(8,128)} async-done(((f32[768,2]{1,0:T(8,128)}), f32[48,2]{1,0:T(8,128)}) %reduce-scatter.33.cloned.1.call-update) | async-done | bytes 400
  1009.0 182.4 %all-reduce.9.cloned.1.call-done = f32[3,768,384]{2,0,1:T(4,128)} async-done(((f32[3,768,384]{2,0,1:T(4,128)}), f32[3,768,384]{2,0,1:T(4,128)}) %all-reduce.9.cloned.1.call-update) | async-done | bytes 3538960
  1193.0 77.6 %reduce-scatter.27.cloned.1.call-done = bf16[2,192,3072]{2,1,0:T(8,128)(2,1)} async-done(((bf16[2,768,3072]{2,1,0:T(8,128)(2,1)}), bf16[2,192,3072]{2,1,0:T(8,128)(2,1)}) %reduce-scatter.27.cloned.1.call-update) | async-done | bytes 2359312 | tf_op jit(solution)/shard_map/reduce_scatter | solution.py:249
  1270.7 4.4 convert_element_type.226
  1275.1 76.0 %reduce-scatter.29.cloned.1.call-done = bf16[2,768,768]{2,1,0:T(8,128)(2,1)} async-done(((bf16[2,3072,768]{2,1,0:T(8,128)(2,1)}), bf16[2,768,768]{2,1,0:T(8,128)(2,1)}) %reduce-scatter.29.cloned.1.call-update) | async-done | bytes 2359312 | tf_op jit(solution)/shard_map/reduce_scatter | solution.py:252
  1355.3 126.0 %reduce-scatter.25.cloned.1.call-done = f32[384,48]{0,1:T(8,128)} async-done(((f32[384,768]{0,1:T(8,128)}), f32[384,48]{0,1:T(8,128)}) %reduce-scatter.25.cloned.1.call-update) | async-done | bytes 73744 | tf_op jit(solution)/shard_map/reduce_scatter | solution.py:312
  (337 shorter events, 244.9 us)
Async XLA Ops:
  8.0 51.7 %copy-start = (bf16[1,1,1280,768]{3,2,1,0:T(8,128)(2,1)S(1)}, bf16[1,1,1280,768]{3,2,1,0:T(8,128)(2,1)}, u32[]{:S(2)}) copy-start(bf16[1,1,1280,768]{3,2,1,0:T(8,128)(2,1)} %param.16) | copy-start | bytes 5898244
  8.0 51.7 %all-gather.12.cloned.1.call-start = ((), (), s32[]{:S(2)}) async-start(), calls=%async_computation.15 | async-start | bytes 1990656 | tf_op jit(solution)/shard_map/all_gather | solution.py:45
  8.8 84.2 %all-gather.22.cloned.1.call-start = ((), (), s32[]{:S(2)}) async-start(), calls=%async_computation.27 | async-start | bytes 2359296 | tf_op jit(solution)/shard_map/all_gather | solution.py:140
  10.2 53.8 %copy-start.27 = (f32[768]{0:T(1024)}, f32[768]{0:T(1024)S(1)}, u32[]{:S(2)}) copy-start(f32[768]{0:T(1024)S(1)} %get-tuple-element.307) | copy-start | bytes 9220
  10.2 53.8 %copy-start.39 = (f32[768]{0:T(1024)}, f32[768]{0:T(1024)S(1)}, u32[]{:S(2)}) copy-start(f32[768]{0:T(1024)S(1)} %get-tuple-element.233) | copy-start | bytes 9220
  12.1 52.0 %copy-start.20 = (f32[1280]{0:T(1024)}, f32[1280]{0:T(1024)S(1)}, u32[]{:S(2)}) copy-start(f32[1280]{0:T(1024)S(1)} %broadcast_multiply_fusion.5) | copy-start | bytes 15364
  14.4 49.7 %copy-start.22 = (f32[1280]{0:T(1024)}, f32[1280]{0:T(1024)S(1)}, u32[]{:S(2)}) copy-start(f32[1280]{0:T(1024)S(1)} %add_rsqrt_fusion.1) | copy-start | bytes 15364
  67.0 8.7 slice-start
  67.1 55.3 %all-gather.24.cloned.1.call-start = ((), (), s32[]{:S(2)}) async-start(), calls=%async_computation.28 | async-start | bytes 2359296 | tf_op jit(solution)/shard_map/all_gather | solution.py:141
  68.7 143.7 %all-to-all-start = ((bf16[8,384,96]{1,2,0:T(8,128)(2,1)}), bf16[8,384,96]{1,2,0:T(8,128)(2,1)}, u32[]{:S(2)}, u32[]{:S(2)}) async-start(bf16[8,384,96]{1,2,0:T(8,128)(2,1)} %stack.16), calls=%async_computation | async-start | bytes 1179648 | tf_op jit(solution)/shard_map/all_to_all | solution.py:47
  72.9 166.8 %all-reduce.5.cloned.1.call-start = ((), (), s32[]{:S(2)}) async-start(), calls=%async_computation.16 | async-start | bytes 3932160 | tf_op jit(solution)/shard_map/psum | solution.py:67
  218.0 21.7 %copy-start.1 = (bf16[1,1,1280,768]{3,2,1,0:T(8,128)(2,1)S(1)}, bf16[1,1,1280,768]{3,2,1,0:T(8,128)(2,1)}, u32[]{:S(2)}) copy-start(bf16[1,1,1280,768]{3,2,1,0:T(8,128)(2,1)} %param.16) | copy-start | bytes 5898244
  218.0 88.3 %all-gather.14.cloned.1.call-start = ((), (), s32[]{:S(2)}) async-start(), calls=%async_computation.17 | async-start | bytes 11796480 | tf_op jit(solution)/shard_map/all_gather | solution.py:54
  218.6 131.4 %all-gather.16.cloned.1.call-start = ((), (), s32[]{:S(2)}) async-start(), calls=%async_computation.18 | async-start | bytes 11796480 | tf_op jit(solution)/shard_map/all_gather | solution.py:55
  221.1 49.8 %copy-start.41 = (s32[640]{0:T(1024)}, s32[640]{0:T(1024)S(1)}, u32[]{:S(2)}) copy-start(s32[640]{0:T(1024)S(1)} %multiply_add_fusion) | copy-start | bytes 7684
  248.6 11.1 copy-start.48
  248.6 16.4 %copy-start.49 = (bf16[2,192]{1,0:T(2,128)(2,1)S(1)}, bf16[2,192]{1,0:T(2,128)(2,1)}, u32[]{:S(2)}) copy-start(bf16[2,192]{1,0:T(2,128)(2,1)} %param.26) | copy-start | bytes 2308
  248.6 22.3 %copy-start.12 = (bf16[1,1,1280,768]{3,2,1,0:T(8,128)(2,1)S(1)}, bf16[1,1,1280,768]{3,2,1,0:T(8,128)(2,1)}, u32[]{:S(2)}) copy-start(bf16[1,1,1280,768]{3,2,1,0:T(8,128)(2,1)} %param.17) | copy-start | bytes 5898244
  248.6 51.6 %all-to-all-start.1 = ((bf16[8,2,80,768]{3,2,1,0:T(8,128)(2,1)}), bf16[8,2,80,768]{3,2,1,0:T(8,128)(2,1)}, u32[]{:S(2)}, u32[]{:S(2)}) async-start(bf16[8,2,80,768]{3,2,1,0:T(8,128)(2,1)} %bitcast.384), calls=%async_computation.1 | async-start | bytes 3932160 | tf_op jit(solution)/shard_map/all_to_all | solution.py:182
  300.2 49.7 %all-to-all-start.3 = ((bf16[8,2,80,768]{3,2,1,0:T(8,128)(2,1)}), bf16[8,2,80,768]{3,2,1,0:T(8,128)(2,1)S(1)}, u32[]{:S(2)}, u32[]{:S(2)}) async-start(bf16[8,2,80,768]{3,2,1,0:T(8,128)(2,1)} %bitcast.383), calls=%async_computation.3 | async-start | bytes 3932160 | tf_op jit(solution)/shard_map/all_to_all | solution.py:219
  303.9 157.8 %all-gather.20.cloned.1.call-start = ((), (), s32[]{:S(2)}) async-start(), calls=%async_computation.20 | async-start | bytes 2949120 | tf_op jit(solution)/shard_map/all_gather | solution.py:63
  306.3 57.6 %copy-start.31 = (f32[8,2,80]{2,0,1:T(8,128)}, f32[8,2,80]{2,0,1:T(8,128)S(1)}, u32[]{:S(2)}) copy-start(f32[8,2,80]{2,0,1:T(8,128)S(1)} %divide_bitcast_fusion) | copy-start | bytes 15364
  350.0 13.9 copy-start.9
  363.9 23.0 %copy-start.38 = (f32[2,768]{1,0:T(2,128)S(1)}, f32[2,768]{1,0:T(2,128)}, u32[]{:S(2)}) copy-start(f32[2,768]{1,0:T(2,128)} %bitcast_convert_fusion.4) | copy-start | bytes 18436
  398.3 51.4 %copy-start.42 = (s32[640]{0:T(1024)S(1)}, s32[640]{0:T(1024)}, u32[]{:S(2)}) copy-start(s32[640]{0:T(1024)} %copy-done.41) | copy-start | bytes 7684
  449.7 11.9 copy-start.30
  449.7 16.7 %copy-start.13 = (bf16[1,1,1280,768]{3,2,1,0:T(8,128)(2,1)S(1)}, bf16[1,1,1280,768]{3,2,1,0:T(8,128)(2,1)}, u32[]{:S(2)}) copy-start(bf16[1,1,1280,768]{3,2,1,0:T(8,128)(2,1)} %param.17) | copy-start | bytes 5898244
  452.4 14.0 copy-start.26
  452.4 193.0 %reduce-scatter.23.cloned.1.call-start = ((), (), s32[]{:S(2)}) async-start(), calls=%async_computation.22 | async-start | bytes 2359296 | tf_op jit(solution)/shard_map/reduce_scatter | solution.py:290
  618.0 56.5 %reduce-scatter.21.cloned.1.call-start = ((), (), s32[]{:S(2)}) async-start(), calls=%async_computation.21 | async-start | bytes 2359296 | tf_op jit(solution)/shard_map/reduce_scatter | solution.py:287
  621.3 9.5 copy-start.19
  622.7 63.6 %all-to-all-start.2 = ((bf16[8,2,80,768]{3,2,1,0:T(8,128)(2,1)}), bf16[8,2,80,768]{3,2,1,0:T(8,128)(2,1)}, u32[]{:S(2)}, u32[]{:S(2)}) async-start(bf16[8,2,80,768]{3,2,1,0:T(8,128)(2,1)} %copy.89), calls=%async_computation.2 | async-start | bytes 3932160 | tf_op jit(solution)/shard_map/all_to_all | solution.py:193
  628.5 73.3 %all-reduce.7.cloned.1.call-start = ((), (), s32[]{:S(2)}) async-start(), calls=%async_computation.23 | async-start | bytes 3932160 | tf_op jit(solution)/shard_map/psum | solution.py:67
  680.6 72.0 %reduce-scatter.37.cloned.1.call-start = ((), (), s32[]{:S(2)}) async-start(), calls=%async_computation.32 | async-start | bytes 245760
  682.0 72.1 %reduce-scatter.39.cloned.1.call-start = ((), (), s32[]{:S(2)}) async-start(), calls=%async_computation.33 | async-start | bytes 245760
  685.0 70.6 %reduce-scatter.35.cloned.1.call-start = ((), (), s32[]{:S(2)}) async-start(), calls=%async_computation.31 | async-start | bytes 983040
  686.3 71.0 %all-gather.18.cloned.1.call-start = ((), (), s32[]{:S(2)}) async-start(), calls=%async_computation.19 | async-start | bytes 2949120 | tf_op jit(solution)/shard_map/all_gather | solution.py:63
  686.4 15.4 %copy-start.2 = (bf16[1,1,1280,768]{3,2,1,0:T(8,128)(2,1)S(1)}, bf16[1,1,1280,768]{3,2,1,0:T(8,128)(2,1)}, u32[]{:S(2)}) copy-start(bf16[1,1,1280,768]{3,2,1,0:T(8,128)(2,1)} %param.16) | copy-start | bytes 5898244
  686.4 15.4 %copy-start.21 = (f32[1280]{0:T(1024)S(1)}, f32[1280]{0:T(1024)}, u32[]{:S(2)}) copy-start(f32[1280]{0:T(1024)} %copy-done.20) | copy-start | bytes 15364
  686.4 15.4 %copy-start.23 = (f32[1280]{0:T(1024)S(1)}, f32[1280]{0:T(1024)}, u32[]{:S(2)}) copy-start(f32[1280]{0:T(1024)} %copy-done.22) | copy-start | bytes 15364
  686.4 15.4 %copy-start.28 = (f32[768]{0:T(1024)S(1)}, f32[768]{0:T(1024)}, u32[]{:S(2)}) copy-start(f32[768]{0:T(1024)} %copy-done.27) | copy-start | bytes 9220
  690.8 16.5 %copy-start.40 = (f32[768]{0:T(1024)S(1)}, f32[768]{0:T(1024)}, u32[]{:S(2)}) copy-start(f32[768]{0:T(1024)} %copy-done.39) | copy-start | bytes 9220
  690.8 190.0 %reduce-scatter.31.cloned.1.call-start = ((), (), s32[]{:S(2)}) async-start(), calls=%async_computation.29 | async-start | bytes 417792
  706.2 301.4 %reduce-scatter.33.cloned.1.call-start = ((), (), s32[]{:S(2)}) async-start(), calls=%async_computation.30 | async-start | bytes 417792
  707.2 484.1 %all-reduce.9.cloned.1.call-start = ((), (), s32[]{:S(2)}) async-start(), calls=%async_computation.34 | async-start | bytes 9437184
  719.5 551.2 %reduce-scatter.27.cloned.1.call-start = ((), (), s32[]{:S(2)}) async-start(), calls=%async_computation.25 | async-start | bytes 11796480 | tf_op jit(solution)/shard_map/reduce_scatter | solution.py:249
  732.5 618.6 %reduce-scatter.29.cloned.1.call-start = ((), (), s32[]{:S(2)}) async-start(), calls=%async_computation.26 | async-start | bytes 11796480 | tf_op jit(solution)/shard_map/reduce_scatter | solution.py:252
  745.8 735.5 %reduce-scatter.25.cloned.1.call-start = ((), (), s32[]{:S(2)}) async-start(), calls=%async_computation.24 | async-start | bytes 1253376 | tf_op jit(solution)/shard_map/reduce_scatter | solution.py:312
  (38 other events, 118.6 us)
Sparse Core Ops, SparseCore 0:
  11.0 48.6 all-gather.11
  67.2 25.7 all-gather.21
  95.1 27.1 all-gather.23
  218.2 21.4 all-reduce.4
  452.5 9.0 all-gather.19
  618.1 27.3 reduce-scatter.22
  648.3 26.1 reduce-scatter.20
  680.7 21.0 all-reduce.6
  703.4 11.5 all-gather.17
Sparse Core Ops, SparseCore 1:
  220.1 64.2 all-gather.13
  285.7 64.1 all-gather.15
  684.1 19.7 reduce-scatter.36
  706.4 20.7 reduce-scatter.38
  729.7 23.1 reduce-scatter.34
  757.5 123.2 reduce-scatter.30
  885.3 122.2 reduce-scatter.32
  1013.8 177.5 all-reduce.8
  1193.8 76.8 reduce-scatter.26
  1273.3 77.8 reduce-scatter.28
  1356.3 124.9 reduce-scatter.24
